TPU v7x, 32 devices: a whole 2x2x4 slice. The times are simulated.
32 devices in a mesh: groups: 2 (over y), shard: 16 (over z, x, core).
Axes of the slice: x: 2, y: 2, z: 4, core: 2. Of those that a mesh axis runs over, the one named last changes fastest.
Arguments:
- query_tokens: bfloat16 [1024, 32, 128], P(('groups', 'shard')), parts along dimension 0, may hold values from -0.1875 to 0.1875
- candidates: int32 [1024, 24], P(('groups', 'shard')), parts along dimension 0, may hold values from 0 to 511, as said below
- cand_count: int32 [1024], P(('groups', 'shard')), parts along dimension 0, may hold values from 3 to 24, as said below
- placement_map: int32 [1024], P('groups'), parts along dimension 0, may hold values from 0 to 511, as said below
- passage_base: bfloat16 [1024, 128, 128], P(('groups', 'shard')), parts along dimension 0, may hold values from -6 to 6
- residual_codes: int32 [1024, 128, 128], P(('groups', 'shard')), parts along dimension 0, may hold values from 0 to 3
- passage_lengths: int32 [1024], P(('groups', 'shard')), parts along dimension 0, may hold values from 32 to 128
- bucket_weights: float32 [8], P('groups'), parts along dimension 0, may hold values from -3 to 3
Outputs:
- scores: float32 [1024, 24], P(('groups', 'shard')), parts along dimension 0
There are 2 independent parts, one for each index of `groups`. A program takes and returns all parts, laid end to end along the dimension named above; each array names one. Nothing has to cross between parts.
Inputs may be any that keep to these rules, and one draw needn't show every extreme that they name: In row q the first cand_count[q] entries are distinct passage ids; the devices that store them (device placement_map[id] // 32 of the shard axis) are at most 3, and one device stores at most 8 of them. Of the 32 queries of one device, one storing device (the same for all devices) holds candidates of exactly 9, and every other storing device holds candidates of at most 6. Entries at or beyond cand_count[q] are arbitrary ids. `cand_count`: entries of candidates at or beyond this count are not scored. A permutation: passage id p is row placement_map[p] of the passage store.
All inputs are finite; a program needn't handle non-finite values.
Results may differ from a plain program's by a relative error of at most 0.0003.
Values may be sent and summed in bfloat16 or wider, within the bound.
A program may use at most 64 MiB of HBM per device.

v0:
```python
import jax
import jax.numpy as jnp
from jax import lax
from jax.sharding import PartitionSpec as P

OWNERS_Q = 3
CPQ = 8
epsilon = 1e-06
negative = -1e30


def decode(bases, code_ids, levels):
    residual = jnp.zeros(bases.shape, jnp.float32)
    for bucket in range(4):
        residual = residual + jnp.where(code_ids == bucket, levels[bucket], 0.0)
    summed = bases.astype(jnp.float32) + residual
    inverse_norm = lax.rsqrt(jnp.sum(summed * summed, axis=-1, keepdims=True) + epsilon)
    return (summed * inverse_norm).astype(jnp.bfloat16)


def score_block(query_rows, token_rows, lengths):
    similarity_scores = jnp.einsum(
        "mqd,mkpd->mqkp", query_rows, token_rows, preferred_element_type=jnp.float32
    )
    inside = (
        jnp.arange(token_rows.shape[2], dtype=jnp.int32)[None, None, None, :]
        < lengths[:, None, :, None]
    )
    maxima = jnp.max(jnp.where(inside, similarity_scores, negative), axis=3)
    return jnp.sum(maxima, axis=1)


def score_slots(query_rows, wanted, decoded, lengths):
    item_count = query_rows.shape[0]
    group_size = 16
    padding = -item_count % group_size
    wanted = jnp.maximum(wanted, 0)
    blocks = (item_count + padding) // group_size

    def one_block(bundle):
        query_part, row_part = bundle
        return score_block(query_part, decoded[row_part], lengths[row_part])

    result = lax.map(
        one_block,
        (
            query_rows.reshape(blocks, group_size, query_rows.shape[1], query_rows.shape[2]),
            wanted.reshape(blocks, group_size, wanted.shape[1]),
        ),
    )
    return result.reshape(blocks * group_size, wanted.shape[1])


def pack(present, holder, capacity, query_tokens):
    present_int = present.astype(jnp.int32)
    slot_of = jnp.cumsum(present_int, axis=0) - present_int
    selection_mask = present.T[:, None, :] & (
        slot_of.T[:, None, :] == jnp.arange(capacity, dtype=jnp.int32)[None, :, None]
    )
    outgoing = jnp.einsum(
        "ksq,qtd->kstd",
        selection_mask.astype(jnp.bfloat16),
        query_tokens,
        preferred_element_type=jnp.float32,
    ).astype(jnp.bfloat16)
    target = (
        jnp.sum(
            selection_mask[:, :, :, None].astype(jnp.int32)
            * (jnp.transpose(holder, (1, 0, 2))[:, None, :, :] + 1),
            axis=2,
        )
        - 1
    )
    return (outgoing, target, slot_of)


def local(
    query_tokens,
    candidates,
    cand_count,
    placement_map,
    passage_base,
    residual_codes,
    passage_lengths,
    bucket_weights,
):
    device_count = lax.axis_size("shard")
    query_count, slot_count = candidates.shape
    store_rows = passage_base.shape[0]
    hot_cap = query_count * OWNERS_Q // device_count + 3
    decoded = decode(passage_base, residual_codes, bucket_weights)
    usable = jnp.arange(slot_count, dtype=jnp.int32)[None, :] < cand_count[:, None]
    stored = placement_map[candidates]
    holders = stored // store_rows
    local_row = stored % store_rows
    shared = usable[:, :, None] & usable[:, None, :] & (holders[:, :, None] == holders[:, None, :])
    preceding_total = (
        jnp.arange(slot_count, dtype=jnp.int32)[None, :]
        < jnp.arange(slot_count, dtype=jnp.int32)[:, None]
    )
    within = jnp.sum((shared & preceding_total[None, :, :]).astype(jnp.int32), axis=2)
    owner_ids = jnp.arange(device_count, dtype=jnp.int32)
    matches = usable[:, :, None] & (holders[:, :, None] == owner_ids[None, None, :])
    present = jnp.any(matches, axis=1)
    rank_ids = jnp.arange(CPQ, dtype=jnp.int32)
    holder = (
        jnp.sum(
            jnp.where(
                matches[:, :, :, None]
                & (within[:, :, None, None] == rank_ids[None, None, None, :]),
                local_row[:, :, None, None] + 1,
                0,
            ),
            axis=1,
        )
        - 1
    )
    outgoing, target, slot_of = pack(present, holder, hot_cap, query_tokens)
    queries_in = lax.all_to_all(outgoing, "shard", split_axis=0, concat_axis=0, tiled=True)
    rows_in = lax.all_to_all(
        target.astype(jnp.bfloat16), "shard", split_axis=0, concat_axis=0, tiled=True
    )
    senders = rows_in.shape[0]
    slots_in = rows_in.shape[1]
    flat_queries = queries_in.reshape(senders * slots_in, queries_in.shape[2], queries_in.shape[3])
    row_list_flat = rows_in.astype(jnp.int32).reshape(senders * slots_in, rows_in.shape[2])
    visited = score_slots(flat_queries, row_list_flat, decoded, passage_lengths).reshape(
        senders, slots_in, rows_in.shape[2]
    )
    returned = lax.all_to_all(visited, "shard", split_axis=0, concat_axis=0, tiled=True)
    flattened = returned.reshape(-1)
    pick_slot = jnp.take_along_axis(slot_of, jnp.clip(holders, 0, device_count - 1), axis=1)
    position = holders * (hot_cap * CPQ) + pick_slot * CPQ + within
    result = jnp.take(flattened, position, mode="clip")
    return jnp.where(usable, result, 0.0)


def solution(mesh):
    return jax.shard_map(
        local,
        mesh=mesh,
        in_specs=(
            P(("groups", "shard"), None, None),
            P(("groups", "shard"), None),
            P(("groups", "shard")),
            P("groups"),
            P(("groups", "shard"), None, None),
            P(("groups", "shard"), None, None),
            P(("groups", "shard")),
            P("groups"),
        ),
        out_specs=P(("groups", "shard"), None),
        check_vma=False,
    )
```

profile of v0, /device:TPU:0, one launch (start us, length us, event | category | flops | bytes accessed | tf_op | source)
XLA Modules:
  0.0 154.1 jit_solution(14491903596649840008)
XLA Ops:
  0.0 0.7 iota_compare_fusion.4
  0.8 0.7 compare_select_fusion.2
  1.8 5.0 %gather_fusion.2 = s32[768]{0:T(1024)S(1)} fusion(s32[512]{0:T(512)S(1)} %copy-done, s32[1024]{0:T(1024)S(1)} %pad_clamp_fusion.2), kind=kCustom, calls=%fused_computation.2 | custom fusion | bytes 9216 | tf_op jit(solution)/shard_map/gather | solution.py:93
  7.0 0.2 convert_reduce_fusion
  7.5 0.3 select_reduce_fusion.1
  7.8 2.5 %multiply_reduce_fusion.1 = s32[16,9,8]{2,1,0:T(8,128)S(1)} fusion(s32[16,32,8]{1,2,0:T(8,128)S(1)} %bitcast.58, s32[16,9,32]{2,1,0:T(8,128)S(1)} %copy.110), kind=kLoop, calls=%fused_computation.18 | loop fusion | flops 72576 | bytes 39424 | tf_op jit(solution)/shard_map/reduce_sum | solution.py:67
  10.3 0.1 copy.113
  10.5 0.7 copy.114
  11.2 7.4 %all-to-all-start = ((bf16[16,9,8]{1,2,0:T(8,128)(2,1)}), bf16[16,9,8]{1,2,0:T(8,128)(2,1)S(1)}, u32[]{:S(2)}, u32[]{:S(2)}) async-start(bf16[16,9,8]{1,2,0:T(8,128)(2,1)} %copy.114), calls=%async_computation | async-start | bytes 65536 | tf_op jit(solution)/shard_map/all_to_all | solution.py:120
  18.6 0.5 convolution_convert_fusion
  19.1 1.3 copy.118
  20.4 4.9 %all-to-all-done = bf16[16,9,8]{1,2,0:T(8,128)(2,1)S(1)} async-done(((bf16[16,9,8]{1,2,0:T(8,128)(2,1)}), bf16[16,9,8]{1,2,0:T(8,128)(2,1)S(1)}, u32[]{:S(2)}, u32[]{:S(2)}) %all-to-all-start) | async-done | bytes 2336 | tf_op jit(solution)/shard_map/all_to_all | solution.py:120
  25.2 4.4 %all-to-all-start.1 = ((bf16[16,9,32,128]{3,2,1,0:T(8,128)(2,1)}), bf16[16,9,32,128]{3,2,1,0:T(8,128)(2,1)}, u32[]{:S(2)}, u32[]{:S(2)}) async-start(bf16[16,9,32,128]{3,2,1,0:T(8,128)(2,1)} %copy.118), calls=%async_computation.1 | async-start | bytes 2359296 | tf_op jit(solution)/shard_map/all_to_all | solution.py:119
  30.0 5.1 %gather_fusion.4 = s32[768]{0:T(1024)S(1)} fusion(s32[32,16]{1,0:T(8,128)S(1)} %convert_subtract_fusion, s32[768]{0:T(1024)S(1)} %reshape.292), kind=kCustom, calls=%fused_computation.4 | custom fusion | bytes 12288 | tf_op jit(solution)/shard_map/jit(take_along_axis)/gather | solution.py:132
  35.5 0.6 fusion.18
  36.2 4.8 %multiply_reduce_fusion = f32[32,128]{1,0:T(8,128)S(1)} fusion(f32[]{:T(128)} %bitcast.17, s32[32,128,128]{2,1,0:T(8,128)S(1)} %copy-done.2, f32[]{:T(128)} %bitcast.16, f32[]{:T(128)} %bitcast.15, f32[]{:T(128)} %bitcast.14, bf16[32,128,128]{2,1,0:T(8,128)(2,1)} %param.14), kind=kLoop, calls=%fused_computation.14 | loop fusion | flops 7860224 | bytes 3162128 | tf_op jit(solution)/shard_map/reduce_sum | solution.py:17
  41.0 4.6 %multiply_convert_fusion = bf16[32,128,128]{2,1,0:T(8,128)(2,1)S(1)} fusion(f32[32,128]{1,0:T(8,128)S(1)} %add_rsqrt_fusion, f32[]{:T(128)} %bitcast.17, s32[32,128,128]{2,1,0:T(8,128)S(1)} %copy-done.2, f32[]{:T(128)} %bitcast.16, f32[]{:T(128)} %bitcast.15, f32[]{:T(128)} %bitcast.14, bf16[32,128,128]{2,1,0:T(8,128)(2,1)} %param.14), kind=kLoop, calls=%fused_computation.13 | loop fusion | flops 7864320 | bytes 4210704 | tf_op jit(solution)/shard_map/convert_element_type | solution.py:18
  45.6 0.1 copy.115
  45.8 0.1 copy.116
  45.9 0.1 max.16
  46.0 8.7 %all-to-all-done.1 = bf16[16,9,32,128]{3,2,1,0:T(8,128)(2,1)} async-done(((bf16[16,9,32,128]{3,2,1,0:T(8,128)(2,1)}), bf16[16,9,32,128]{3,2,1,0:T(8,128)(2,1)}, u32[]{:S(2)}, u32[]{:S(2)}) %all-to-all-start.1) | async-done | bytes 1179680 | tf_op jit(solution)/shard_map/all_to_all | solution.py:119
  54.7 78.7 %while.10 = (s32[]{:T(128)}, f32[9,16,8]{1,0,2:T(8,128)S(1)}, s32[9,16,8]{1,0,2:T(8,128)S(1)}, s32[32]{0:T(128)S(1)}, bf16[9,16,32,128]{3,2,1,0:T(8,128)(2,1)}, ...) while((s32[]{:T(128)}, f32[9,16,8]{1,0,2:T(8,128)S(1)}, ...), condition=%wide.region_9.10_spmd, body=%wide.region_6.9_spmd.sunk | while | flops 135283968 | bytes 12794485 | solution.py:44
  54.9 1.2 gather_fusion.1
  56.2 0.1 iota_compare_fusion.7
  56.3 3.0 %gather_fusion = bf16[128,128,128]{2,1,0:T(8,128)(2,1)} fusion(bf16[32,128,128]{2,1,0:T(8,128)(2,1)S(1)} %get-tuple-element.148, s32[1024]{0:T(1024)S(1)} %pad_clamp_fusion.4), kind=kCustom, calls=%fused_computation.1.clone.1 | custom fusion | bytes 8389120 | tf_op jit(solution)/shard_map/while/body/eval_jaxpr/gather | solution.py:42
  59.3 3.9 %select_reduce_fusion.3 = f32[16,32,8]{1,2,0:T(8,128)S(1)} fusion(bf16[16,8,128,128]{3,2,1,0:T(8,128)(2,1)} %bitcast.55, pred[16,8,128]{2,1,0:T(8,128)(4,1)S(1)} %iota_compare_fusion.7, bf16[9,16,32,128]{3,2,1,0:T(8,128)(2,1)} %get-tuple-element.147, s32[]{:T(128)S(6)} %copy.149), kind=kOutput, calls=%fused_computation.5.clone.1 | convolution fusion | flops 135262208 | bytes 4358148 | tf_op jit(solution)/shard_map/while/body/eval_jaxpr/mqd,mkpd->mqkp/dot_general | solution.py:22
  63.6 1.2 gather_fusion.1
  64.9 0.1 iota_compare_fusion.7
  65.0 3.0 %gather_fusion = bf16[128,128,128]{2,1,0:T(8,128)(2,1)} fusion(bf16[32,128,128]{2,1,0:T(8,128)(2,1)S(1)} %get-tuple-element.148, s32[1024]{0:T(1024)S(1)} %pad_clamp_fusion.4), kind=kCustom, calls=%fused_computation.1.clone.1 | custom fusion | bytes 8389120 | tf_op jit(solution)/shard_map/while/body/eval_jaxpr/gather | solution.py:42
  68.1 3.9 %select_reduce_fusion.3 = f32[16,32,8]{1,2,0:T(8,128)S(1)} fusion(bf16[16,8,128,128]{3,2,1,0:T(8,128)(2,1)} %bitcast.55, pred[16,8,128]{2,1,0:T(8,128)(4,1)S(1)} %iota_compare_fusion.7, bf16[9,16,32,128]{3,2,1,0:T(8,128)(2,1)} %get-tuple-element.147, s32[]{:T(128)S(6)} %copy.149), kind=kOutput, calls=%fused_computation.5.clone.1 | convolution fusion | flops 135262208 | bytes 4358148 | tf_op jit(solution)/shard_map/while/body/eval_jaxpr/mqd,mkpd->mqkp/dot_general | solution.py:22
  72.4 1.2 gather_fusion.1
  73.7 0.1 iota_compare_fusion.7
  73.8 3.0 %gather_fusion = bf16[128,128,128]{2,1,0:T(8,128)(2,1)} fusion(bf16[32,128,128]{2,1,0:T(8,128)(2,1)S(1)} %get-tuple-element.148, s32[1024]{0:T(1024)S(1)} %pad_clamp_fusion.4), kind=kCustom, calls=%fused_computation.1.clone.1 | custom fusion | bytes 8389120 | tf_op jit(solution)/shard_map/while/body/eval_jaxpr/gather | solution.py:42
  76.8 3.9 %select_reduce_fusion.3 = f32[16,32,8]{1,2,0:T(8,128)S(1)} fusion(bf16[16,8,128,128]{3,2,1,0:T(8,128)(2,1)} %bitcast.55, pred[16,8,128]{2,1,0:T(8,128)(4,1)S(1)} %iota_compare_fusion.7, bf16[9,16,32,128]{3,2,1,0:T(8,128)(2,1)} %get-tuple-element.147, s32[]{:T(128)S(6)} %copy.149), kind=kOutput, calls=%fused_computation.5.clone.1 | convolution fusion | flops 135262208 | bytes 4358148 | tf_op jit(solution)/shard_map/while/body/eval_jaxpr/mqd,mkpd->mqkp/dot_general | solution.py:22
  81.1 1.2 gather_fusion.1
  82.4 0.1 iota_compare_fusion.7
  82.5 3.0 %gather_fusion = bf16[128,128,128]{2,1,0:T(8,128)(2,1)} fusion(bf16[32,128,128]{2,1,0:T(8,128)(2,1)S(1)} %get-tuple-element.148, s32[1024]{0:T(1024)S(1)} %pad_clamp_fusion.4), kind=kCustom, calls=%fused_computation.1.clone.1 | custom fusion | bytes 8389120 | tf_op jit(solution)/shard_map/while/body/eval_jaxpr/gather | solution.py:42
  85.6 3.9 %select_reduce_fusion.3 = f32[16,32,8]{1,2,0:T(8,128)S(1)} fusion(bf16[16,8,128,128]{3,2,1,0:T(8,128)(2,1)} %bitcast.55, pred[16,8,128]{2,1,0:T(8,128)(4,1)S(1)} %iota_compare_fusion.7, bf16[9,16,32,128]{3,2,1,0:T(8,128)(2,1)} %get-tuple-element.147, s32[]{:T(128)S(6)} %copy.149), kind=kOutput, calls=%fused_computation.5.clone.1 | convolution fusion | flops 135262208 | bytes 4358148 | tf_op jit(solution)/shard_map/while/body/eval_jaxpr/mqd,mkpd->mqkp/dot_general | solution.py:22
  89.9 1.2 gather_fusion.1
  91.3 3.0 %gather_fusion = bf16[128,128,128]{2,1,0:T(8,128)(2,1)} fusion(bf16[32,128,128]{2,1,0:T(8,128)(2,1)S(1)} %get-tuple-element.148, s32[1024]{0:T(1024)S(1)} %pad_clamp_fusion.4), kind=kCustom, calls=%fused_computation.1.clone.1 | custom fusion | bytes 8389120 | tf_op jit(solution)/shard_map/while/body/eval_jaxpr/gather | solution.py:42
  94.3 3.9 %select_reduce_fusion.3 = f32[16,32,8]{1,2,0:T(8,128)S(1)} fusion(bf16[16,8,128,128]{3,2,1,0:T(8,128)(2,1)} %bitcast.55, pred[16,8,128]{2,1,0:T(8,128)(4,1)S(1)} %iota_compare_fusion.7, bf16[9,16,32,128]{3,2,1,0:T(8,128)(2,1)} %get-tuple-element.147, s32[]{:T(128)S(6)} %copy.149), kind=kOutput, calls=%fused_computation.5.clone.1 | convolution fusion | flops 135262208 | bytes 4358148 | tf_op jit(solution)/shard_map/while/body/eval_jaxpr/mqd,mkpd->mqkp/dot_general | solution.py:22
  98.6 1.2 gather_fusion.1
  99.9 0.1 iota_compare_fusion.7
  100.0 3.0 %gather_fusion = bf16[128,128,128]{2,1,0:T(8,128)(2,1)} fusion(bf16[32,128,128]{2,1,0:T(8,128)(2,1)S(1)} %get-tuple-element.148, s32[1024]{0:T(1024)S(1)} %pad_clamp_fusion.4), kind=kCustom, calls=%fused_computation.1.clone.1 | custom fusion | bytes 8389120 | tf_op jit(solution)/shard_map/while/body/eval_jaxpr/gather | solution.py:42
  103.1 3.9 %select_reduce_fusion.3 = f32[16,32,8]{1,2,0:T(8,128)S(1)} fusion(bf16[16,8,128,128]{3,2,1,0:T(8,128)(2,1)} %bitcast.55, pred[16,8,128]{2,1,0:T(8,128)(4,1)S(1)} %iota_compare_fusion.7, bf16[9,16,32,128]{3,2,1,0:T(8,128)(2,1)} %get-tuple-element.147, s32[]{:T(128)S(6)} %copy.149), kind=kOutput, calls=%fused_computation.5.clone.1 | convolution fusion | flops 135262208 | bytes 4358148 | tf_op jit(solution)/shard_map/while/body/eval_jaxpr/mqd,mkpd->mqkp/dot_general | solution.py:22
  107.4 1.2 gather_fusion.1
  108.7 0.1 iota_compare_fusion.7
  108.8 3.0 %gather_fusion = bf16[128,128,128]{2,1,0:T(8,128)(2,1)} fusion(bf16[32,128,128]{2,1,0:T(8,128)(2,1)S(1)} %get-tuple-element.148, s32[1024]{0:T(1024)S(1)} %pad_clamp_fusion.4), kind=kCustom, calls=%fused_computation.1.clone.1 | custom fusion | bytes 8389120 | tf_op jit(solution)/shard_map/while/body/eval_jaxpr/gather | solution.py:42
  111.8 3.9 %select_reduce_fusion.3 = f32[16,32,8]{1,2,0:T(8,128)S(1)} fusion(bf16[16,8,128,128]{3,2,1,0:T(8,128)(2,1)} %bitcast.55, pred[16,8,128]{2,1,0:T(8,128)(4,1)S(1)} %iota_compare_fusion.7, bf16[9,16,32,128]{3,2,1,0:T(8,128)(2,1)} %get-tuple-element.147, s32[]{:T(128)S(6)} %copy.149), kind=kOutput, calls=%fused_computation.5.clone.1 | convolution fusion | flops 135262208 | bytes 4358148 | tf_op jit(solution)/shard_map/while/body/eval_jaxpr/mqd,mkpd->mqkp/dot_general | solution.py:22
  116.1 1.2 gather_fusion.1
  117.4 0.1 iota_compare_fusion.7
  117.5 3.0 %gather_fusion = bf16[128,128,128]{2,1,0:T(8,128)(2,1)} fusion(bf16[32,128,128]{2,1,0:T(8,128)(2,1)S(1)} %get-tuple-element.148, s32[1024]{0:T(1024)S(1)} %pad_clamp_fusion.4), kind=kCustom, calls=%fused_computation.1.clone.1 | custom fusion | bytes 8389120 | tf_op jit(solution)/shard_map/while/body/eval_jaxpr/gather | solution.py:42
  120.6 3.9 %select_reduce_fusion.3 = f32[16,32,8]{1,2,0:T(8,128)S(1)} fusion(bf16[16,8,128,128]{3,2,1,0:T(8,128)(2,1)} %bitcast.55, pred[16,8,128]{2,1,0:T(8,128)(4,1)S(1)} %iota_compare_fusion.7, bf16[9,16,32,128]{3,2,1,0:T(8,128)(2,1)} %get-tuple-element.147, s32[]{:T(128)S(6)} %copy.149), kind=kOutput, calls=%fused_computation.5.clone.1 | convolution fusion | flops 135262208 | bytes 4358148 | tf_op jit(solution)/shard_map/while/body/eval_jaxpr/mqd,mkpd->mqkp/dot_general | solution.py:22
  124.9 1.2 gather_fusion.1
  126.2 0.1 iota_compare_fusion.7
  126.3 3.0 %gather_fusion = bf16[128,128,128]{2,1,0:T(8,128)(2,1)} fusion(bf16[32,128,128]{2,1,0:T(8,128)(2,1)S(1)} %get-tuple-element.148, s32[1024]{0:T(1024)S(1)} %pad_clamp_fusion.4), kind=kCustom, calls=%fused_computation.1.clone.1 | custom fusion | bytes 8389120 | tf_op jit(solution)/shard_map/while/body/eval_jaxpr/gather | solution.py:42
  129.3 3.9 %select_reduce_fusion.3 = f32[16,32,8]{1,2,0:T(8,128)S(1)} fusion(bf16[16,8,128,128]{3,2,1,0:T(8,128)(2,1)} %bitcast.55, pred[16,8,128]{2,1,0:T(8,128)(4,1)S(1)} %iota_compare_fusion.7, bf16[9,16,32,128]{3,2,1,0:T(8,128)(2,1)} %get-tuple-element.147, s32[]{:T(128)S(6)} %copy.149), kind=kOutput, calls=%fused_computation.5.clone.1 | convolution fusion | flops 135262208 | bytes 4358148 | tf_op jit(solution)/shard_map/while/body/eval_jaxpr/mqd,mkpd->mqkp/dot_general | solution.py:22
  133.5 0.6 copy.121
  134.2 7.4 %all-to-all-start.2 = ((f32[16,9,8]{1,2,0:T(8,128)}), f32[16,9,8]{1,2,0:T(8,128)S(1)}, u32[]{:S(2)}, u32[]{:S(2)}) async-start(f32[16,9,8]{1,2,0:T(8,128)} %copy.121), calls=%async_computation.2 | async-start | bytes 131072 | tf_op jit(solution)/shard_map/all_to_all | solution.py:130
  141.6 6.9 %all-to-all-done.2 = f32[16,9,8]{1,2,0:T(8,128)S(1)} async-done(((f32[16,9,8]{1,2,0:T(8,128)}), f32[16,9,8]{1,2,0:T(8,128)S(1)}, u32[]{:S(2)}, u32[]{:S(2)}) %all-to-all-start.2) | async-done | bytes 4640 | tf_op jit(solution)/shard_map/all_to_all | solution.py:130
  148.5 0.2 copy.122
  148.6 0.1 reshape.259
  148.7 4.5 %gather_fusion.3 = f32[768]{0:T(1024)S(1)} fusion(f32[1152]{0:T(1024)S(1)} %reshape.259, s32[1024]{0:T(1024)S(1)} %pad_clamp_fusion.1), kind=kCustom, calls=%fused_computation.3 | custom fusion | bytes 9216 | tf_op jit(solution)/shard_map/jit(_take)/gather | solution.py:134
  153.4 0.7 copy.130
  (130 shorter events, 5.9 us)
Async XLA Ops:
  0.0 1.7 %copy-start = (s32[512]{0:T(512)S(1)}, s32[512]{0:T(512)}, u32[]{:S(2)}) copy-start(s32[512]{0:T(512)} %param.13) | copy-start | bytes 6148
  1.7 16.9 %copy-start.3 = (bf16[32,32,128]{2,1,0:T(8,128)(2,1)S(1)}, bf16[32,32,128]{2,1,0:T(8,128)(2,1)}, u32[]{:S(2)}) copy-start(bf16[32,32,128]{2,1,0:T(8,128)(2,1)} %param.10) | copy-start | bytes 786436
  11.2 14.0 %all-to-all-start = ((bf16[16,9,8]{1,2,0:T(8,128)(2,1)}), bf16[16,9,8]{1,2,0:T(8,128)(2,1)S(1)}, u32[]{:S(2)}, u32[]{:S(2)}) async-start(bf16[16,9,8]{1,2,0:T(8,128)(2,1)} %copy.114), calls=%async_computation | async-start | bytes 65536 | tf_op jit(solution)/shard_map/all_to_all | solution.py:120
  25.2 29.5 %all-to-all-start.1 = ((bf16[16,9,32,128]{3,2,1,0:T(8,128)(2,1)}), bf16[16,9,32,128]{3,2,1,0:T(8,128)(2,1)}, u32[]{:S(2)}, u32[]{:S(2)}) async-start(bf16[16,9,32,128]{3,2,1,0:T(8,128)(2,1)} %copy.118), calls=%async_computation.1 | async-start | bytes 2359296 | tf_op jit(solution)/shard_map/all_to_all | solution.py:119
  30.0 5.5 %copy-start.4 = (f32[4]{0:T(128)S(1)}, f32[4]{0:T(128)}, u32[]{:S(2)}) copy-start(f32[4]{0:T(128)} %param.17) | copy-start | bytes 52
  30.0 6.2 %copy-start.2 = (s32[32,128,128]{2,1,0:T(8,128)S(1)}, s32[32,128,128]{2,1,0:T(8,128)}, u32[]{:S(2)}) copy-start(s32[32,128,128]{2,1,0:T(8,128)} %param.15) | copy-start | bytes 6291460
  41.0 13.7 %copy-start.1 = (s32[32]{0:T(128)S(1)}, s32[32]{0:T(128)}, u32[]{:S(2)}) copy-start(s32[32]{0:T(128)} %param.16) | copy-start | bytes 388
  134.2 14.3 %all-to-all-start.2 = ((f32[16,9,8]{1,2,0:T(8,128)}), f32[16,9,8]{1,2,0:T(8,128)S(1)}, u32[]{:S(2)}, u32[]{:S(2)}) async-start(f32[16,9,8]{1,2,0:T(8,128)} %copy.121), calls=%async_computation.2 | async-start | bytes 131072 | tf_op jit(solution)/shard_map/all_to_all | solution.py:130
  148.7 4.6 %copy-start.5 = (s32[32]{0:T(128)S(1)}, s32[32]{0:T(128)}, u32[]{:S(2)}) copy-start(s32[32]{0:T(128)} %param.12) | copy-start | bytes 388
where the time goes:
time: 155 us; the launch traced here: 154 us
  local copies, waits for them, and re-layouts  62 us (40%)
  matrix products  35.5 us (23%)
  waiting for transfers between devices  20.4 us (13%)
  starting transfers between devices  19.2 us (12%)
  other arithmetic  16 us (10%)
    gather x27, local copies, waits for them, and re-layouts, one_block(): return score_block(query_part, decoded[row_part], lengths[row_part])  38.8 us
    dot_general x9, matrix products, score_block(): jnp.einsum('mqd,mkpd->mqkp', query_rows, token_rows, preferred_element_ty...  35 us
    all_to_all x1, waiting for transfers between devices, local(): lax.all_to_all(outgoing, 'shard', split_axis=0, concat_axis=0, tiled=True)  8.68 us
    all_to_all x1, starting transfers between devices, local(): lax.all_to_all(visited, 'shard', split_axis=0, concat_axis=0, tiled=True)  7.39 us
    all_to_all x1, starting transfers between devices, local(): lax.all_to_all(target.astype(jnp.bfloat16), 'shard', split_axis=0, concat...  7.39 us
    all_to_all x1, waiting for transfers between devices, local(): lax.all_to_all(visited, 'shard', split_axis=0, concat_axis=0, tiled=True)  6.88 us
    gather x5, local copies, waits for them, and re-layouts, local(): jnp.take_along_axis(slot_of, jnp.clip(holders, 0, device_count - 1), axis=1)  5.46 us
    gather x5, local copies, waits for them, and re-layouts, local(): stored = placement_map[candidates]  5.3 us
  transfers between devices with their start and end apart: 3, of which 3 were waited for; matrix products, arithmetic and copies ran while one was open for 12% of the time, Pallas kernels for 0%

commit v1 on v0

--- a/solution.py
+++ b/solution.py
@@ -7,6 +7,28 @@
 CPQ = 8
 epsilon = 1e-06
 negative = -1e30
+
+
+def cut_along(x, dim, size):
+    before, after = (x.shape[:dim], x.shape[dim + 1 :])
+    return jnp.moveaxis(x.reshape(*before, size, -1, *after), dim, 0)
+
+
+def laid_out(blocks, dim):
+    shape = list(blocks.shape[1:])
+    shape[dim] *= blocks.shape[0]
+    return jnp.moveaxis(blocks, 0, dim).reshape(shape)
+
+
+def exchange_in_pairs(shard, axis, split_dim, concat_dim):
+    length, here = (lax.axis_size(axis), lax.axis_index(axis))
+    pieces = cut_along(shard, split_dim, length)
+    outs = [pieces[here]]
+    for step in range(1, length):
+        sent = pieces[here ^ step]
+        outs.append(lax.ppermute(sent, axis, [(i, i ^ step) for i in range(length)]))
+    pieces = jnp.stack(outs)[here ^ jnp.arange(length)]
+    return laid_out(pieces, concat_dim)
 
 
 def decode(bases, code_ids, levels):
@@ -116,7 +138,7 @@
         - 1
     )
     outgoing, target, slot_of = pack(present, holder, hot_cap, query_tokens)
-    queries_in = lax.all_to_all(outgoing, "shard", split_axis=0, concat_axis=0, tiled=True)
+    queries_in = exchange_in_pairs(outgoing, "shard", 0, 0)
     rows_in = lax.all_to_all(
         target.astype(jnp.bfloat16), "shard", split_axis=0, concat_axis=0, tiled=True
     )

time: 155 us -> 238 us (1.54)
  waiting for transfers between devices: 20.4 us -> 72.9 us
  local copies, waits for them, and re-layouts: 62 us -> 83.6 us
  starting transfers between devices: 19.2 us -> 27.7 us
    ppermute x0 -> x15, waiting for transfers between devices: none -> 66 us  [exchange_in_pairs(): lax.ppermute(sent, axis, [(i, i ^ step) for i in range(length)])]
    ppermute x0 -> x15, starting transfers between devices: none -> 16.8 us  [exchange_in_pairs(): lax.ppermute(sent, axis, [(i, i ^ step) for i in range(length)])]
    dynamic_update_slice x9, local copies, waits for them, and re-layouts: 0.26 us -> 12.5 us  [score_slots(): lax.map(one_block, (query_rows.reshape(blocks, group_size, query_rows.sha...]
    all_to_all x1 -> x0, waiting for transfers between devices: 8.68 us -> none  [local(): lax.all_to_all(outgoing, 'shard', split_axis=0, concat_axis=0, tiled=True)]
    all_to_all x1, waiting for transfers between devices: 4.85 us -> 0.01 us  [local(): lax.all_to_all(target.astype(jnp.bfloat16), 'shard', split_axis=0, concat...]
    all_to_all x1 -> x0, starting transfers between devices: 4.39 us -> none  [local(): lax.all_to_all(outgoing, 'shard', split_axis=0, concat_axis=0, tiled=True)]
    unnamed x12 -> x43, local copies, waits for them, and re-layouts: 0.04 us -> 4 us
    squeeze x0 -> x1, local copies, waits for them, and re-layouts: none -> 3.94 us  [exchange_in_pairs(): sent = pieces[here ^ step]]
  transfers between devices with their start and end apart: 3 -> 17, of which waited for: 3 -> 11; matrix products, arithmetic and copies ran while one was open for 12% -> 10% of each run, Pallas kernels for 0% -> 0%
where the time goes in v1:
time: 238 us; the launch traced here: 236 us
  local copies, waits for them, and re-layouts  83.6 us (35%)
  waiting for transfers between devices  72.9 us (31%)
  matrix products  34.8 us (15%)
  starting transfers between devices  27.7 us (12%)
  other arithmetic  16 us (7%)
    ppermute x15, waiting for transfers between devices, exchange_in_pairs(): lax.ppermute(sent, axis, [(i, i ^ step) for i in range(length)])  66 us
    gather x27, local copies, waits for them, and re-layouts, one_block(): return score_block(query_part, decoded[row_part], lengths[row_part])  39 us
    dot_general x9, matrix products, score_block(): jnp.einsum('mqd,mkpd->mqkp', query_rows, token_rows, preferred_element_ty...  34.3 us
    ppermute x15, starting transfers between devices, exchange_in_pairs(): lax.ppermute(sent, axis, [(i, i ^ step) for i in range(length)])  16.8 us
    dynamic_update_slice x9, local copies, waits for them, and re-layouts, score_slots(): lax.map(one_block, (query_rows.reshape(blocks, group_size, query_rows.sha...  12.5 us
    all_to_all x1, starting transfers between devices, local(): lax.all_to_all(target.astype(jnp.bfloat16), 'shard', split_axis=0, concat...  7.39 us
    all_to_all x1, waiting for transfers between devices, local(): lax.all_to_all(visited, 'shard', split_axis=0, concat_axis=0, tiled=True)  6.85 us
    gather x5, local copies, waits for them, and re-layouts, local(): jnp.take_along_axis(slot_of, jnp.clip(holders, 0, device_count - 1), axis=1)  5.46 us
  transfers between devices with their start and end apart: 17, of which 11 were waited for; matrix products, arithmetic and copies ran while one was open for 10% of the time, Pallas kernels for 0%

profile of v1, /device:TPU:0, one launch (start us, length us, event | category | flops | bytes accessed | tf_op | source)
XLA Modules:
  0.0 236.0 jit_solution(537959871928346469)
XLA Ops:
  1.7 5.0 %gather_fusion.2 = s32[768]{0:T(1024)S(1)} fusion(s32[512]{0:T(512)S(1)} %copy-done, s32[1024]{0:T(1024)S(1)} %pad_clamp_fusion.3), kind=kCustom, calls=%fused_computation.2 | custom fusion | bytes 9216 | tf_op jit(solution)/shard_map/gather | solution.py:115
  7.8 2.5 %multiply_reduce_fusion.1 = s32[16,9,8]{2,1,0:T(8,128)S(1)} fusion(s32[16,32,8]{1,2,0:T(8,128)S(1)} %bitcast.95, s32[16,9,32]{2,1,0:T(8,128)S(1)} %copy.379), kind=kLoop, calls=%fused_computation.19 | loop fusion | flops 72576 | bytes 39424 | tf_op jit(solution)/shard_map/reduce_sum | solution.py:89
  11.2 7.4 %all-to-all-start = ((bf16[16,9,8]{1,2,0:T(8,128)(2,1)}), bf16[16,9,8]{1,2,0:T(8,128)(2,1)S(1)}, u32[]{:S(2)}, u32[]{:S(2)}) async-start(bf16[16,9,8]{1,2,0:T(8,128)(2,1)} %copy.383), calls=%async_computation | async-start | bytes 65536 | tf_op jit(solution)/shard_map/all_to_all | solution.py:142
  19.2 3.9 %constant_dynamic-slice_fusion.1 = (bf16[1,9,32,128]{3,0,2,1:T(2,128)(2,1)}, bf16[1,9,32,128]{3,0,2,1:T(2,128)(2,1)}, bf16[1,9,32,128]{3,0,2,1:T(2,128)(2,1)}, b...) fusion(bf16[16,9,32,128]{3,0,2,1:T(8,128)(2,1)S(1)} %convolutio, ...), kind=kLoop, calls=%fused_computation.79 | loop fusion | bytes 2359360 | tf_op jit(solution)/shard_map/squeeze | solution.py:28
  23.2 4.3 %collective-permute-start.14 = (bf16[1,9,32,128]{3,0,2,1:T(2,128)(2,1)}, bf16[1,9,32,128]{3,0,2,1:T(2,128)(2,1)}, u32[]{:S(2)}, u32[]{:S(2)}) collective-permute-start(bf16[1,9,32,128]{3,0,2,1:T(2,128)(2,1)} %get-tuple-element.164), channel_id=1, source_target_pairs={{0,15},{1,14},{2,13},{3,12},{4,11},{5,10},{6,9},{7,8},{8,7},{9,6},... | collective-permute-start | bytes 221192 | tf_op jit(solution)/shard_map/ppermute | solution.py:29
  27.9 3.2 %collective-permute-start.12 = (bf16[1,9,32,128]{3,0,2,1:T(2,128)(2,1)}, bf16[1,9,32,128]{3,0,2,1:T(2,128)(2,1)}, u32[]{:S(2)}, u32[]{:S(2)}) collective-permute-start(bf16[1,9,32,128]{3,0,2,1:T(2,128)(2,1)} %get-tuple-element.166), channel_id=1, source_target_pairs={{0,13},{1,12},{2,15},{3,14},{4,9},{5,8},{6,11},{7,10},{8,5},{9,4},... | collective-permute-start | bytes 221192 | tf_op jit(solution)/shard_map/ppermute | solution.py:29
  32.5 4.8 %multiply_reduce_fusion = f32[32,128]{1,0:T(8,128)S(1)} fusion(f32[]{:T(128)} %bitcast.19, s32[32,128,128]{2,1,0:T(8,128)S(1)} %copy-done.2, f32[]{:T(128)} %bitcast.18, f32[]{:T(128)} %bitcast.17, f32[]{:T(128)} %bitcast.16, bf16[32,128,128]{2,1,0:T(8,128)(2,1)} %param.14), kind=kLoop, calls=%fused_computation.15 | loop fusion | flops 7860224 | bytes 3162128 | tf_op jit(solution)/shard_map/reduce_sum | solution.py:39
  37.3 5.1 %gather_fusion.5 = s32[768]{0:T(1024)S(1)} fusion(s32[32,16]{1,0:T(8,128)S(1)} %convert_subtract_fusion, s32[768]{0:T(1024)S(1)} %reshape.350), kind=kCustom, calls=%fused_computation.5 | custom fusion | bytes 12288 | tf_op jit(solution)/shard_map/jit(take_along_axis)/gather | solution.py:154
  42.7 4.6 %multiply_convert_fusion = bf16[32,128,128]{2,1,0:T(8,128)(2,1)S(1)} fusion(f32[32,128]{1,0:T(8,128)S(1)} %add_rsqrt_fusion, f32[]{:T(128)} %bitcast.19, s32[32,128,128]{2,1,0:T(8,128)S(1)} %copy-done.2, f32[]{:T(128)} %bitcast.18, f32[]{:T(128)} %bitcast.17, f32[]{:T(128)} %bitcast.16, bf16[32,128,128]{2,1,0:T(8,128)(2,1)} %param.14), kind=kLoop, calls=%fused_computation.14 | loop fusion | flops 7864320 | bytes 4210704 | tf_op jit(solution)/shard_map/convert_element_type | solution.py:40
  48.0 1.7 collective-permute-start.1
  50.6 3.7 %collective-permute-done.1 = bf16[1,9,32,128]{3,0,2,1:T(2,128)(2,1)S(1)} collective-permute-done((bf16[1,9,32,128]{3,0,2,1:T(2,128)(2,1)}, bf16[1,9,32,128]{3,0,2,1:T(2,128)(2,1)S(1)}, u32[]{:S(2)}, u32[]{:S(2)}) %collective-permute-start.1) | collective-permute-done | bytes 73760 | tf_op jit(solution)/shard_map/ppermute | solution.py:29
  55.2 5.2 %collective-permute-done.2 = bf16[1,9,32,128]{3,0,2,1:T(2,128)(2,1)S(1)} collective-permute-done((bf16[1,9,32,128]{3,0,2,1:T(2,128)(2,1)}, bf16[1,9,32,128]{3,0,2,1:T(2,128)(2,1)S(1)}, u32[]{:S(2)}, u32[]{:S(2)}) %collective-permute-start.2) | collective-permute-done | bytes 73760 | tf_op jit(solution)/shard_map/ppermute | solution.py:29
  60.4 6.1 %collective-permute-done.3 = bf16[1,9,32,128]{3,0,2,1:T(2,128)(2,1)S(1)} collective-permute-done((bf16[1,9,32,128]{3,0,2,1:T(2,128)(2,1)}, bf16[1,9,32,128]{3,0,2,1:T(2,128)(2,1)S(1)}, u32[]{:S(2)}, u32[]{:S(2)}) %collective-permute-start.3) | collective-permute-done | bytes 73760 | tf_op jit(solution)/shard_map/ppermute | solution.py:29
  66.5 5.6 %collective-permute-done.4 = bf16[1,9,32,128]{3,0,2,1:T(2,128)(2,1)S(1)} collective-permute-done((bf16[1,9,32,128]{3,0,2,1:T(2,128)(2,1)S(1)}, bf16[1,9,32,128]{3,0,2,1:T(2,128)(2,1)S(1)}, u32[]{:S(2)}, u32[]{:S(2)}) %collective-permute-start.4) | collective-permute-done | bytes 73760 | tf_op jit(solution)/shard_map/ppermute | solution.py:29
  72.0 1.5 collective-permute-start.5
  73.5 4.7 %collective-permute-done.5 = bf16[1,9,32,128]{3,0,2,1:T(2,128)(2,1)S(1)} collective-permute-done((bf16[1,9,32,128]{3,0,2,1:T(2,128)(2,1)S(1)}, bf16[1,9,32,128]{3,0,2,1:T(2,128)(2,1)S(1)}, u32[]{:S(2)}, u32[]{:S(2)}) %collective-permute-start.5) | collective-permute-done | bytes 73760 | tf_op jit(solution)/shard_map/ppermute | solution.py:29
  79.2 5.8 %collective-permute-done.6 = bf16[1,9,32,128]{3,0,2,1:T(2,128)(2,1)S(1)} collective-permute-done((bf16[1,9,32,128]{3,0,2,1:T(2,128)(2,1)S(1)}, bf16[1,9,32,128]{3,0,2,1:T(2,128)(2,1)S(1)}, u32[]{:S(2)}, u32[]{:S(2)}) %collective-permute-start.6) | collective-permute-done | bytes 73760 | tf_op jit(solution)/shard_map/ppermute | solution.py:29
  85.0 3.2 %collective-permute-start.7 = (bf16[1,9,32,128]{3,0,2,1:T(2,128)(2,1)S(1)}, bf16[1,9,32,128]{3,0,2,1:T(2,128)(2,1)S(1)}, u32[]{:S(2)}, u32[]{:S(2)}) collective-permute-start(bf16[1,9,32,128]{3,0,2,1:T(2,128)(2,1)S(1)} %copy-done.8), channel_id=1, source_target_pairs={{0,8},{1,9},{2,10},{3,11},{4,12},{5,13},{6,14},{7,15},{8,0},{9,1},... | collective-permute-start | bytes 221192 | tf_op jit(solution)/shard_map/ppermute | solution.py:29
  88.2 6.4 %collective-permute-done.7 = bf16[1,9,32,128]{3,0,2,1:T(2,128)(2,1)S(1)} collective-permute-done((bf16[1,9,32,128]{3,0,2,1:T(2,128)(2,1)S(1)}, bf16[1,9,32,128]{3,0,2,1:T(2,128)(2,1)S(1)}, u32[]{:S(2)}, u32[]{:S(2)}) %collective-permute-start.7) | collective-permute-done | bytes 73760 | tf_op jit(solution)/shard_map/ppermute | solution.py:29
  94.7 9.4 %collective-permute-done.8 = bf16[1,9,32,128]{3,0,2,1:T(2,128)(2,1)S(1)} collective-permute-done((bf16[1,9,32,128]{3,0,2,1:T(2,128)(2,1)S(1)}, bf16[1,9,32,128]{3,0,2,1:T(2,128)(2,1)S(1)}, u32[]{:S(2)}, u32[]{:S(2)}) %collective-permute-start.8) | collective-permute-done | bytes 73760 | tf_op jit(solution)/shard_map/ppermute | solution.py:29
  104.4 8.8 %collective-permute-done.9 = bf16[1,9,32,128]{3,0,2,1:T(2,128)(2,1)S(1)} collective-permute-done((bf16[1,9,32,128]{3,0,2,1:T(2,128)(2,1)S(1)}, bf16[1,9,32,128]{3,0,2,1:T(2,128)(2,1)S(1)}, u32[]{:S(2)}, u32[]{:S(2)}) %collective-permute-start.9) | collective-permute-done | bytes 73760 | tf_op jit(solution)/shard_map/ppermute | solution.py:29
  113.3 10.3 %collective-permute-done.10 = bf16[1,9,32,128]{3,0,2,1:T(2,128)(2,1)S(1)} collective-permute-done((bf16[1,9,32,128]{3,0,2,1:T(2,128)(2,1)S(1)}, bf16[1,9,32,128]{3,0,2,1:T(2,128)(2,1)S(1)}, u32[]{:S(2)}, u32[]{:S(2)}) %collective-permute-start.10) | collective-permute-done | bytes 73760 | tf_op jit(solution)/shard_map/ppermute | solution.py:29
  125.5 0.9 bitcast_dynamic-update-slice_fusion.1
  128.2 90.2 %while.10 = (s32[]{:T(128)}, f32[9,16,8]{1,0,2:T(8,128)}, s32[9,16,8]{1,0,2:T(8,128)S(1)}, s32[32]{0:T(128)S(1)}, bf16[9,16,32,128]{3,2,1,0:T(8,128)(2,1)S(1)}, ...) while((s32[]{:T(128)}, f32[9,16,8]{1,0,2:T(8,128)}, s32[9,16,8]{1,0,2:T(8,128)S(1)}, ...), condition=%wide.region_9.10_spmd, body=%wide.region_6.9_spmd.sunk | while | flops 135283968 | bytes 12794485 | solution.py:66
  128.4 1.2 gather_fusion.1
  129.8 3.0 %gather_fusion = bf16[128,128,128]{2,1,0:T(8,128)(2,1)} fusion(bf16[32,128,128]{2,1,0:T(8,128)(2,1)S(1)} %get-tuple-element.248, s32[1024]{0:T(1024)S(1)} %pad_clamp_fusion.5), kind=kCustom, calls=%fused_computation.1.clone.1 | custom fusion | bytes 8389120 | tf_op jit(solution)/shard_map/while/body/eval_jaxpr/gather | solution.py:64
  132.9 3.8 %select_reduce_fusion.3 = f32[16,32,8]{1,2,0:T(8,128)S(1)} fusion(bf16[16,8,128,128]{3,2,1,0:T(8,128)(2,1)} %bitcast.90, pred[16,8,128]{2,1,0:T(8,128)(4,1)S(1)} %iota_compare_fusion.7, bf16[9,16,32,128]{3,2,1,0:T(8,128)(2,1)S(1)} %get-tuple-element.247, s32[]{:T(128)S(6)} %copy.464), kind=kOutput, calls=%fused_computation.6.clone.1 | convolution fusion | flops 135262208 | bytes 4358148 | tf_op jit(solution)/shard_map/while/body/eval_jaxpr/mqd,mkpd->mqkp/dot_general | solution.py:44
  136.9 1.4 dynamic_update_slice.5
  138.4 1.2 gather_fusion.1
  139.9 3.0 %gather_fusion = bf16[128,128,128]{2,1,0:T(8,128)(2,1)} fusion(bf16[32,128,128]{2,1,0:T(8,128)(2,1)S(1)} %get-tuple-element.248, s32[1024]{0:T(1024)S(1)} %pad_clamp_fusion.5), kind=kCustom, calls=%fused_computation.1.clone.1 | custom fusion | bytes 8389120 | tf_op jit(solution)/shard_map/while/body/eval_jaxpr/gather | solution.py:64
  142.9 3.8 %select_reduce_fusion.3 = f32[16,32,8]{1,2,0:T(8,128)S(1)} fusion(bf16[16,8,128,128]{3,2,1,0:T(8,128)(2,1)} %bitcast.90, pred[16,8,128]{2,1,0:T(8,128)(4,1)S(1)} %iota_compare_fusion.7, bf16[9,16,32,128]{3,2,1,0:T(8,128)(2,1)S(1)} %get-tuple-element.247, s32[]{:T(128)S(6)} %copy.464), kind=kOutput, calls=%fused_computation.6.clone.1 | convolution fusion | flops 135262208 | bytes 4358148 | tf_op jit(solution)/shard_map/while/body/eval_jaxpr/mqd,mkpd->mqkp/dot_general | solution.py:44
  146.9 1.4 dynamic_update_slice.5
  148.5 1.2 gather_fusion.1
  149.9 3.0 %gather_fusion = bf16[128,128,128]{2,1,0:T(8,128)(2,1)} fusion(bf16[32,128,128]{2,1,0:T(8,128)(2,1)S(1)} %get-tuple-element.248, s32[1024]{0:T(1024)S(1)} %pad_clamp_fusion.5), kind=kCustom, calls=%fused_computation.1.clone.1 | custom fusion | bytes 8389120 | tf_op jit(solution)/shard_map/while/body/eval_jaxpr/gather | solution.py:64
  152.9 3.8 %select_reduce_fusion.3 = f32[16,32,8]{1,2,0:T(8,128)S(1)} fusion(bf16[16,8,128,128]{3,2,1,0:T(8,128)(2,1)} %bitcast.90, pred[16,8,128]{2,1,0:T(8,128)(4,1)S(1)} %iota_compare_fusion.7, bf16[9,16,32,128]{3,2,1,0:T(8,128)(2,1)S(1)} %get-tuple-element.247, s32[]{:T(128)S(6)} %copy.464), kind=kOutput, calls=%fused_computation.6.clone.1 | convolution fusion | flops 135262208 | bytes 4358148 | tf_op jit(solution)/shard_map/while/body/eval_jaxpr/mqd,mkpd->mqkp/dot_general | solution.py:44
  156.9 1.4 dynamic_update_slice.5
  158.5 1.2 gather_fusion.1
  159.9 3.0 %gather_fusion = bf16[128,128,128]{2,1,0:T(8,128)(2,1)} fusion(bf16[32,128,128]{2,1,0:T(8,128)(2,1)S(1)} %get-tuple-element.248, s32[1024]{0:T(1024)S(1)} %pad_clamp_fusion.5), kind=kCustom, calls=%fused_computation.1.clone.1 | custom fusion | bytes 8389120 | tf_op jit(solution)/shard_map/while/body/eval_jaxpr/gather | solution.py:64
  162.9 3.8 %select_reduce_fusion.3 = f32[16,32,8]{1,2,0:T(8,128)S(1)} fusion(bf16[16,8,128,128]{3,2,1,0:T(8,128)(2,1)} %bitcast.90, pred[16,8,128]{2,1,0:T(8,128)(4,1)S(1)} %iota_compare_fusion.7, bf16[9,16,32,128]{3,2,1,0:T(8,128)(2,1)S(1)} %get-tuple-element.247, s32[]{:T(128)S(6)} %copy.464), kind=kOutput, calls=%fused_computation.6.clone.1 | convolution fusion | flops 135262208 | bytes 4358148 | tf_op jit(solution)/shard_map/while/body/eval_jaxpr/mqd,mkpd->mqkp/dot_general | solution.py:44
  166.9 1.4 dynamic_update_slice.5
  168.5 1.2 gather_fusion.1
  169.9 3.0 %gather_fusion = bf16[128,128,128]{2,1,0:T(8,128)(2,1)} fusion(bf16[32,128,128]{2,1,0:T(8,128)(2,1)S(1)} %get-tuple-element.248, s32[1024]{0:T(1024)S(1)} %pad_clamp_fusion.5), kind=kCustom, calls=%fused_computation.1.clone.1 | custom fusion | bytes 8389120 | tf_op jit(solution)/shard_map/while/body/eval_jaxpr/gather | solution.py:64
  173.0 3.8 %select_reduce_fusion.3 = f32[16,32,8]{1,2,0:T(8,128)S(1)} fusion(bf16[16,8,128,128]{3,2,1,0:T(8,128)(2,1)} %bitcast.90, pred[16,8,128]{2,1,0:T(8,128)(4,1)S(1)} %iota_compare_fusion.7, bf16[9,16,32,128]{3,2,1,0:T(8,128)(2,1)S(1)} %get-tuple-element.247, s32[]{:T(128)S(6)} %copy.464), kind=kOutput, calls=%fused_computation.6.clone.1 | convolution fusion | flops 135262208 | bytes 4358148 | tf_op jit(solution)/shard_map/while/body/eval_jaxpr/mqd,mkpd->mqkp/dot_general | solution.py:44
  176.9 1.4 dynamic_update_slice.5
  178.5 1.2 gather_fusion.1
  179.9 3.0 %gather_fusion = bf16[128,128,128]{2,1,0:T(8,128)(2,1)} fusion(bf16[32,128,128]{2,1,0:T(8,128)(2,1)S(1)} %get-tuple-element.248, s32[1024]{0:T(1024)S(1)} %pad_clamp_fusion.5), kind=kCustom, calls=%fused_computation.1.clone.1 | custom fusion | bytes 8389120 | tf_op jit(solution)/shard_map/while/body/eval_jaxpr/gather | solution.py:64
  183.0 3.8 %select_reduce_fusion.3 = f32[16,32,8]{1,2,0:T(8,128)S(1)} fusion(bf16[16,8,128,128]{3,2,1,0:T(8,128)(2,1)} %bitcast.90, pred[16,8,128]{2,1,0:T(8,128)(4,1)S(1)} %iota_compare_fusion.7, bf16[9,16,32,128]{3,2,1,0:T(8,128)(2,1)S(1)} %get-tuple-element.247, s32[]{:T(128)S(6)} %copy.464), kind=kOutput, calls=%fused_computation.6.clone.1 | convolution fusion | flops 135262208 | bytes 4358148 | tf_op jit(solution)/shard_map/while/body/eval_jaxpr/mqd,mkpd->mqkp/dot_general | solution.py:44
  187.0 1.4 dynamic_update_slice.5
  188.6 1.2 gather_fusion.1
  190.0 3.0 %gather_fusion = bf16[128,128,128]{2,1,0:T(8,128)(2,1)} fusion(bf16[32,128,128]{2,1,0:T(8,128)(2,1)S(1)} %get-tuple-element.248, s32[1024]{0:T(1024)S(1)} %pad_clamp_fusion.5), kind=kCustom, calls=%fused_computation.1.clone.1 | custom fusion | bytes 8389120 | tf_op jit(solution)/shard_map/while/body/eval_jaxpr/gather | solution.py:64
  193.0 3.8 %select_reduce_fusion.3 = f32[16,32,8]{1,2,0:T(8,128)S(1)} fusion(bf16[16,8,128,128]{3,2,1,0:T(8,128)(2,1)} %bitcast.90, pred[16,8,128]{2,1,0:T(8,128)(4,1)S(1)} %iota_compare_fusion.7, bf16[9,16,32,128]{3,2,1,0:T(8,128)(2,1)S(1)} %get-tuple-element.247, s32[]{:T(128)S(6)} %copy.464), kind=kOutput, calls=%fused_computation.6.clone.1 | convolution fusion | flops 135262208 | bytes 4358148 | tf_op jit(solution)/shard_map/while/body/eval_jaxpr/mqd,mkpd->mqkp/dot_general | solution.py:44
  197.0 1.4 dynamic_update_slice.5
  198.6 1.2 gather_fusion.1
  200.0 3.0 %gather_fusion = bf16[128,128,128]{2,1,0:T(8,128)(2,1)} fusion(bf16[32,128,128]{2,1,0:T(8,128)(2,1)S(1)} %get-tuple-element.248, s32[1024]{0:T(1024)S(1)} %pad_clamp_fusion.5), kind=kCustom, calls=%fused_computation.1.clone.1 | custom fusion | bytes 8389120 | tf_op jit(solution)/shard_map/while/body/eval_jaxpr/gather | solution.py:64
  203.0 3.8 %select_reduce_fusion.3 = f32[16,32,8]{1,2,0:T(8,128)S(1)} fusion(bf16[16,8,128,128]{3,2,1,0:T(8,128)(2,1)} %bitcast.90, pred[16,8,128]{2,1,0:T(8,128)(4,1)S(1)} %iota_compare_fusion.7, bf16[9,16,32,128]{3,2,1,0:T(8,128)(2,1)S(1)} %get-tuple-element.247, s32[]{:T(128)S(6)} %copy.464), kind=kOutput, calls=%fused_computation.6.clone.1 | convolution fusion | flops 135262208 | bytes 4358148 | tf_op jit(solution)/shard_map/while/body/eval_jaxpr/mqd,mkpd->mqkp/dot_general | solution.py:44
  207.0 1.4 dynamic_update_slice.5
  208.6 1.2 gather_fusion.1
  210.0 3.0 %gather_fusion = bf16[128,128,128]{2,1,0:T(8,128)(2,1)} fusion(bf16[32,128,128]{2,1,0:T(8,128)(2,1)S(1)} %get-tuple-element.248, s32[1024]{0:T(1024)S(1)} %pad_clamp_fusion.5), kind=kCustom, calls=%fused_computation.1.clone.1 | custom fusion | bytes 8389120 | tf_op jit(solution)/shard_map/while/body/eval_jaxpr/gather | solution.py:64
  213.1 3.8 %select_reduce_fusion.3 = f32[16,32,8]{1,2,0:T(8,128)S(1)} fusion(bf16[16,8,128,128]{3,2,1,0:T(8,128)(2,1)} %bitcast.90, pred[16,8,128]{2,1,0:T(8,128)(4,1)S(1)} %iota_compare_fusion.7, bf16[9,16,32,128]{3,2,1,0:T(8,128)(2,1)S(1)} %get-tuple-element.247, s32[]{:T(128)S(6)} %copy.464), kind=kOutput, calls=%fused_computation.6.clone.1 | convolution fusion | flops 135262208 | bytes 4358148 | tf_op jit(solution)/shard_map/while/body/eval_jaxpr/mqd,mkpd->mqkp/dot_general | solution.py:44
  217.0 1.4 dynamic_update_slice.5
  218.4 0.9 reshape_reshape.3
  220.0 3.5 %all-to-all-start.1 = ((f32[16,9,8]{1,2,0:T(8,128)}), f32[16,9,8]{1,2,0:T(8,128)S(1)}, u32[]{:S(2)}, u32[]{:S(2)}) async-start(f32[16,9,8]{1,2,0:T(8,128)} %copy.389), calls=%async_computation.1 | async-start | bytes 131072 | tf_op jit(solution)/shard_map/all_to_all | solution.py:152
  223.5 6.8 %all-to-all-done.1 = f32[16,9,8]{1,2,0:T(8,128)S(1)} async-done(((f32[16,9,8]{1,2,0:T(8,128)}), f32[16,9,8]{1,2,0:T(8,128)S(1)}, u32[]{:S(2)}, u32[]{:S(2)}) %all-to-all-start.1) | async-done | bytes 4640 | tf_op jit(solution)/shard_map/all_to_all | solution.py:152
  230.7 4.5 %gather_fusion.4 = f32[768]{0:T(1024)S(1)} fusion(f32[1152]{0:T(1024)S(1)} %reshape.307, s32[1024]{0:T(1024)S(1)} %pad_clamp_fusion.1), kind=kCustom, calls=%fused_computation.4 | custom fusion | bytes 9216 | tf_op jit(solution)/shard_map/jit(_take)/gather | solution.py:156
  (193 shorter events, 19.9 us)
Async XLA Ops:
  0.0 1.7 copy-start
  6.8 11.9 %copy-start.4 = (bf16[32,32,128]{2,1,0:T(8,128)(2,1)S(1)}, bf16[32,32,128]{2,1,0:T(8,128)(2,1)}, u32[]{:S(2)}) copy-start(bf16[32,32,128]{2,1,0:T(8,128)(2,1)} %param.10) | copy-start | bytes 786436
  11.2 36.4 %all-to-all-start = ((bf16[16,9,8]{1,2,0:T(8,128)(2,1)}), bf16[16,9,8]{1,2,0:T(8,128)(2,1)S(1)}, u32[]{:S(2)}, u32[]{:S(2)}) async-start(bf16[16,9,8]{1,2,0:T(8,128)(2,1)} %copy.383), calls=%async_computation | async-start | bytes 65536 | tf_op jit(solution)/shard_map/all_to_all | solution.py:142
  19.2 12.4 %copy-start.12 = (f32[4]{0:T(128)S(1)}, f32[4]{0:T(128)}, u32[]{:S(2)}) copy-start(f32[4]{0:T(128)} %param.17) | copy-start | bytes 52
  19.2 13.3 %copy-start.2 = (s32[32,128,128]{2,1,0:T(8,128)S(1)}, s32[32,128,128]{2,1,0:T(8,128)}, u32[]{:S(2)}) copy-start(s32[32,128,128]{2,1,0:T(8,128)} %param.15) | copy-start | bytes 6291460
  23.2 103.3 %collective-permute-start.14 = (bf16[1,9,32,128]{3,0,2,1:T(2,128)(2,1)}, bf16[1,9,32,128]{3,0,2,1:T(2,128)(2,1)}, u32[]{:S(2)}, u32[]{:S(2)}) collective-permute-start(bf16[1,9,32,128]{3,0,2,1:T(2,128)(2,1)} %get-tuple-element.164), channel_id=1, source_target_pairs={{0,15},{1,14},{2,13},{3,12},{4,11},{5,10},{6,9},{7,8},{8,7},{9,6},... | collective-permute-start | bytes 221192 | tf_op jit(solution)/shard_map/ppermute | solution.py:29
  27.5 98.1 %collective-permute-start.13 = (bf16[1,9,32,128]{3,0,2,1:T(2,128)(2,1)}, bf16[1,9,32,128]{3,0,2,1:T(2,128)(2,1)}, u32[]{:S(2)}, u32[]{:S(2)}) collective-permute-start(bf16[1,9,32,128]{3,0,2,1:T(2,128)(2,1)} %get-tuple-element.165), channel_id=1, source_target_pairs={{0,14},{1,15},{2,12},{3,13},{4,10},{5,11},{6,8},{7,9},{8,6},{9,7},... | collective-permute-start | bytes 221192 | tf_op jit(solution)/shard_map/ppermute | solution.py:29
  27.9 96.7 %collective-permute-start.12 = (bf16[1,9,32,128]{3,0,2,1:T(2,128)(2,1)}, bf16[1,9,32,128]{3,0,2,1:T(2,128)(2,1)}, u32[]{:S(2)}, u32[]{:S(2)}) collective-permute-start(bf16[1,9,32,128]{3,0,2,1:T(2,128)(2,1)} %get-tuple-element.166), channel_id=1, source_target_pairs={{0,13},{1,12},{2,15},{3,14},{4,9},{5,8},{6,11},{7,10},{8,5},{9,4},... | collective-permute-start | bytes 221192 | tf_op jit(solution)/shard_map/ppermute | solution.py:29
  31.0 92.6 %collective-permute-start.11 = (bf16[1,9,32,128]{3,0,2,1:T(2,128)(2,1)}, bf16[1,9,32,128]{3,0,2,1:T(2,128)(2,1)}, u32[]{:S(2)}, u32[]{:S(2)}) collective-permute-start(bf16[1,9,32,128]{3,0,2,1:T(2,128)(2,1)} %get-tuple-element.167), channel_id=1, source_target_pairs={{0,12},{1,13},{2,14},{3,15},{4,8},{5,9},{6,10},{7,11},{8,4},{9,5},... | collective-permute-start | bytes 221192 | tf_op jit(solution)/shard_map/ppermute | solution.py:29
  31.3 16.7 %collective-permute-start = (bf16[1,9,32,128]{3,0,2,1:T(2,128)(2,1)}, bf16[1,9,32,128]{3,0,2,1:T(2,128)(2,1)}, u32[]{:S(2)}, u32[]{:S(2)}) collective-permute-start(bf16[1,9,32,128]{3,0,2,1:T(2,128)(2,1)} %get-tuple-element.178), channel_id=1, source_target_pairs={{0,1},{1,0},{2,3},{3,2},{4,5},{5,4},{6,7},{7,6},{8,9},{9,8},{10,11... | collective-permute-start | bytes 221192 | tf_op jit(solution)/shard_map/ppermute | solution.py:29
  42.7 4.7 %copy-start.3 = (bf16[1,9,32,128]{3,0,2,1:T(2,128)(2,1)S(1)}, bf16[1,9,32,128]{3,0,2,1:T(2,128)(2,1)}, u32[]{:S(2)}) copy-start(bf16[1,9,32,128]{3,0,2,1:T(2,128)(2,1)} %get-tuple-element.179) | copy-start | bytes 221188
  47.3 19.2 %copy-start.11 = (bf16[1,9,32,128]{3,0,2,1:T(2,128)(2,1)S(1)}, bf16[1,9,32,128]{3,0,2,1:T(2,128)(2,1)}, u32[]{:S(2)}) copy-start(bf16[1,9,32,128]{3,0,2,1:T(2,128)(2,1)} %get-tuple-element.174) | copy-start | bytes 221188
  47.3 24.7 %copy-start.10 = (bf16[1,9,32,128]{3,0,2,1:T(2,128)(2,1)S(1)}, bf16[1,9,32,128]{3,0,2,1:T(2,128)(2,1)}, u32[]{:S(2)}) copy-start(bf16[1,9,32,128]{3,0,2,1:T(2,128)(2,1)} %get-tuple-element.173) | copy-start | bytes 221188
  47.3 30.9 %copy-start.9 = (bf16[1,9,32,128]{3,0,2,1:T(2,128)(2,1)S(1)}, bf16[1,9,32,128]{3,0,2,1:T(2,128)(2,1)}, u32[]{:S(2)}) copy-start(bf16[1,9,32,128]{3,0,2,1:T(2,128)(2,1)} %get-tuple-element.172) | copy-start | bytes 221188
  47.3 37.7 %copy-start.8 = (bf16[1,9,32,128]{3,0,2,1:T(2,128)(2,1)S(1)}, bf16[1,9,32,128]{3,0,2,1:T(2,128)(2,1)}, u32[]{:S(2)}) copy-start(bf16[1,9,32,128]{3,0,2,1:T(2,128)(2,1)} %get-tuple-element.171) | copy-start | bytes 221188
  47.3 47.3 %copy-start.7 = (bf16[1,9,32,128]{3,0,2,1:T(2,128)(2,1)S(1)}, bf16[1,9,32,128]{3,0,2,1:T(2,128)(2,1)}, u32[]{:S(2)}) copy-start(bf16[1,9,32,128]{3,0,2,1:T(2,128)(2,1)} %get-tuple-element.170) | copy-start | bytes 221188
  47.4 56.7 %copy-start.6 = (bf16[1,9,32,128]{3,0,2,1:T(2,128)(2,1)S(1)}, bf16[1,9,32,128]{3,0,2,1:T(2,128)(2,1)}, u32[]{:S(2)}) copy-start(bf16[1,9,32,128]{3,0,2,1:T(2,128)(2,1)} %get-tuple-element.169) | copy-start | bytes 221188
  47.6 65.7 %copy-start.5 = (bf16[1,9,32,128]{3,0,2,1:T(2,128)(2,1)S(1)}, bf16[1,9,32,128]{3,0,2,1:T(2,128)(2,1)}, u32[]{:S(2)}) copy-start(bf16[1,9,32,128]{3,0,2,1:T(2,128)(2,1)} %get-tuple-element.168) | copy-start | bytes 221188
  48.0 6.3 %collective-permute-start.1 = (bf16[1,9,32,128]{3,0,2,1:T(2,128)(2,1)}, bf16[1,9,32,128]{3,0,2,1:T(2,128)(2,1)S(1)}, u32[]{:S(2)}, u32[]{:S(2)}) collective-permute-start(bf16[1,9,32,128]{3,0,2,1:T(2,128)(2,1)} %get-tuple-element.177), channel_id=1, source_target_pairs={{0,2},{1,3},{2,0},{3,1},{4,6},{5,7},{6,4},{7,5},{8,10},{9,11},{10,... | collective-permute-start | bytes 221192 | tf_op jit(solution)/shard_map/ppermute | solution.py:29
  54.3 6.1 %collective-permute-start.2 = (bf16[1,9,32,128]{3,0,2,1:T(2,128)(2,1)}, bf16[1,9,32,128]{3,0,2,1:T(2,128)(2,1)S(1)}, u32[]{:S(2)}, u32[]{:S(2)}) collective-permute-start(bf16[1,9,32,128]{3,0,2,1:T(2,128)(2,1)} %get-tuple-element.176), channel_id=1, source_target_pairs={{0,3},{1,2},{2,1},{3,0},{4,7},{5,6},{6,5},{7,4},{8,11},{9,10},{10,... | collective-permute-start | bytes 221192 | tf_op jit(solution)/shard_map/ppermute | solution.py:29
  60.4 6.1 %collective-permute-start.3 = (bf16[1,9,32,128]{3,0,2,1:T(2,128)(2,1)}, bf16[1,9,32,128]{3,0,2,1:T(2,128)(2,1)S(1)}, u32[]{:S(2)}, u32[]{:S(2)}) collective-permute-start(bf16[1,9,32,128]{3,0,2,1:T(2,128)(2,1)} %get-tuple-element.175), channel_id=1, source_target_pairs={{0,4},{1,5},{2,6},{3,7},{4,0},{5,1},{6,2},{7,3},{8,12},{9,13},{10,... | collective-permute-start | bytes 221192 | tf_op jit(solution)/shard_map/ppermute | solution.py:29
  66.5 5.6 %collective-permute-start.4 = (bf16[1,9,32,128]{3,0,2,1:T(2,128)(2,1)S(1)}, bf16[1,9,32,128]{3,0,2,1:T(2,128)(2,1)S(1)}, u32[]{:S(2)}, u32[]{:S(2)}) collective-permute-start(bf16[1,9,32,128]{3,0,2,1:T(2,128)(2,1)S(1)} %copy-done.11), channel_id=1, source_target_pairs={{0,5},{1,4},{2,7},{3,6},{4,1},{5,0},{6,3},{7,2},{8,13},{9,12},{10,... | collective-permute-start | bytes 221192 | tf_op jit(solution)/shard_map/ppermute | solution.py:29
  72.0 6.2 %collective-permute-start.5 = (bf16[1,9,32,128]{3,0,2,1:T(2,128)(2,1)S(1)}, bf16[1,9,32,128]{3,0,2,1:T(2,128)(2,1)S(1)}, u32[]{:S(2)}, u32[]{:S(2)}) collective-permute-start(bf16[1,9,32,128]{3,0,2,1:T(2,128)(2,1)S(1)} %copy-done.10), channel_id=1, source_target_pairs={{0,6},{1,7},{2,4},{3,5},{4,2},{5,3},{6,0},{7,1},{8,14},{9,15},{10,... | collective-permute-start | bytes 221192 | tf_op jit(solution)/shard_map/ppermute | solution.py:29
  78.3 6.7 %collective-permute-start.6 = (bf16[1,9,32,128]{3,0,2,1:T(2,128)(2,1)S(1)}, bf16[1,9,32,128]{3,0,2,1:T(2,128)(2,1)S(1)}, u32[]{:S(2)}, u32[]{:S(2)}) collective-permute-start(bf16[1,9,32,128]{3,0,2,1:T(2,128)(2,1)S(1)} %copy-done.9), channel_id=1, source_target_pairs={{0,7},{1,6},{2,5},{3,4},{4,3},{5,2},{6,1},{7,0},{8,15},{9,14},{10,... | collective-permute-start | bytes 221192 | tf_op jit(solution)/shard_map/ppermute | solution.py:29
  85.0 9.7 %collective-permute-start.7 = (bf16[1,9,32,128]{3,0,2,1:T(2,128)(2,1)S(1)}, bf16[1,9,32,128]{3,0,2,1:T(2,128)(2,1)S(1)}, u32[]{:S(2)}, u32[]{:S(2)}) collective-permute-start(bf16[1,9,32,128]{3,0,2,1:T(2,128)(2,1)S(1)} %copy-done.8), channel_id=1, source_target_pairs={{0,8},{1,9},{2,10},{3,11},{4,12},{5,13},{6,14},{7,15},{8,0},{9,1},... | collective-permute-start | bytes 221192 | tf_op jit(solution)/shard_map/ppermute | solution.py:29
  94.7 9.4 %collective-permute-start.8 = (bf16[1,9,32,128]{3,0,2,1:T(2,128)(2,1)S(1)}, bf16[1,9,32,128]{3,0,2,1:T(2,128)(2,1)S(1)}, u32[]{:S(2)}, u32[]{:S(2)}) collective-permute-start(bf16[1,9,32,128]{3,0,2,1:T(2,128)(2,1)S(1)} %copy-done.7), channel_id=1, source_target_pairs={{0,9},{1,8},{2,11},{3,10},{4,13},{5,12},{6,15},{7,14},{8,1},{9,0},... | collective-permute-start | bytes 221192 | tf_op jit(solution)/shard_map/ppermute | solution.py:29
  104.1 9.2 %collective-permute-start.9 = (bf16[1,9,32,128]{3,0,2,1:T(2,128)(2,1)S(1)}, bf16[1,9,32,128]{3,0,2,1:T(2,128)(2,1)S(1)}, u32[]{:S(2)}, u32[]{:S(2)}) collective-permute-start(bf16[1,9,32,128]{3,0,2,1:T(2,128)(2,1)S(1)} %copy-done.6), channel_id=1, source_target_pairs={{0,10},{1,11},{2,8},{3,9},{4,14},{5,15},{6,12},{7,13},{8,2},{9,3},... | collective-permute-start | bytes 221192 | tf_op jit(solution)/shard_map/ppermute | solution.py:29
  113.3 10.3 %collective-permute-start.10 = (bf16[1,9,32,128]{3,0,2,1:T(2,128)(2,1)S(1)}, bf16[1,9,32,128]{3,0,2,1:T(2,128)(2,1)S(1)}, u32[]{:S(2)}, u32[]{:S(2)}) collective-permute-start(bf16[1,9,32,128]{3,0,2,1:T(2,128)(2,1)S(1)} %copy-done.5), channel_id=1, source_target_pairs={{0,11},{1,10},{2,9},{3,8},{4,15},{5,14},{6,13},{7,12},{8,3},{9,2},... | collective-permute-start | bytes 221192 | tf_op jit(solution)/shard_map/ppermute | solution.py:29
  127.4 0.8 copy-start.1
  220.0 10.4 %all-to-all-start.1 = ((f32[16,9,8]{1,2,0:T(8,128)}), f32[16,9,8]{1,2,0:T(8,128)S(1)}, u32[]{:S(2)}, u32[]{:S(2)}) async-start(f32[16,9,8]{1,2,0:T(8,128)} %copy.389), calls=%async_computation.1 | async-start | bytes 131072 | tf_op jit(solution)/shard_map/all_to_all | solution.py:152
  230.7 4.6 %copy-start.13 = (s32[32]{0:T(128)S(1)}, s32[32]{0:T(128)}, u32[]{:S(2)}) copy-start(s32[32]{0:T(128)} %param.12) | copy-start | bytes 388
